TPU v7x, 256 devices: a whole 4x4x8 slice. The times are simulated.
256 devices in a mesh: dp: 16 (over x, y), tensor: 16 (over z, core).
Axes of the slice: x: 4, y: 4, z: 8, core: 2. Of those that a mesh axis runs over, the one named last changes fastest.
Arguments:
- tokens: bfloat16 [8192, 8192], P(('dp', 'tensor')), may hold values from -6 to 6
- w_query: bfloat16 [8192, 8192], P(None, 'tensor'), may hold values from -0.0625 to 0.0625
- cotangent: bfloat16 [8192, 8192], P('dp', 'tensor'), may hold values from -6 to 6
- task_embed: bfloat16 [128, 1024], replicated, may hold values from -6 to 6
- w_hidden: bfloat16 [1024, 512], P(None, 'tensor'), may hold values from -0.1875 to 0.1875
- head_a: bfloat16 [512, 16, 8192], P(None, 'dp', 'tensor'), may hold values from -0.0234375 to 0.0234375
- head_b: bfloat16 [512, 16, 8192], P(None, 'dp', 'tensor'), may hold values from -0.0234375 to 0.0234375
- block_task: int32 [16], replicated, may hold values from 0 to 127
Outputs:
- output: bfloat16 [8192, 8192], P('dp', 'tensor')
- grad_tokens: bfloat16 [8192, 8192], P(('dp', 'tensor'))
- grad_head_a: bfloat16 [512, 16, 8192], P(None, 'dp', 'tensor')
- grad_head_b: bfloat16 [512, 16, 8192], P(None, 'dp', 'tensor')
All inputs are finite; a program needn't handle non-finite values.
Results may differ from a plain program's by a relative error of at most 0.0077.
Values may be sent and summed in bfloat16 or wider, within the bound.
No kernel may reach another device: no remote copies, remote signals or barrier semaphores. Data moves between devices by JAX's collectives and lax.ppermute only.
A program may use at most 128 MiB of HBM per device.

v0:
```python
import jax
import jax.numpy as jnp
from jax import lax
from jax.sharding import PartitionSpec as P


def local(tokens, w_query, cotangent, task_embed, w_hidden, head_a, head_b, block_task):
    single_float = jnp.float32
    brain_half_float = jnp.bfloat16
    n_groups = lax.axis_size("dp")
    n_shards = lax.axis_size("tensor")
    shard = lax.axis_index("tensor")
    group = lax.axis_index("dp")
    hid_count, rank_rows, width = head_a.shape
    ntasks = task_embed.shape[0]
    blocks = block_task.shape[0]
    per_group = blocks // n_groups
    hid_part = jax.nn.silu(
        jnp.dot(task_embed, w_hidden, preferred_element_type=single_float)
    ).astype(brain_half_float)
    hidden = lax.all_gather(hid_part, "tensor", axis=1, tiled=True)
    flat_a = head_a.reshape(hid_count, rank_rows * width)
    flat_b = head_b.reshape(hid_count, rank_rows * width)
    mine = lax.dynamic_slice_in_dim(block_task, group * per_group, per_group)
    task_ids = jnp.arange(ntasks, dtype=jnp.int32)
    gen_a = (
        jnp.dot(hidden, flat_a, preferred_element_type=single_float)
        .astype(brain_half_float)
        .reshape(ntasks, rank_rows, width)
    )
    gen_b = (
        jnp.dot(hidden, flat_b, preferred_element_type=single_float)
        .astype(brain_half_float)
        .reshape(ntasks, rank_rows, width)
    )
    all_tasks_down, all_tasks_up = (
        lax.all_gather(gen_a, "dp", axis=1, tiled=True),
        lax.all_gather(gen_b, "dp", axis=1, tiled=True),
    )
    task_selector = (mine[:, None] == task_ids[None, :]).astype(brain_half_float)
    adapter_down_weight = jnp.einsum(
        "yg,ghi->yhi", task_selector, all_tasks_down, preferred_element_type=single_float
    ).astype(brain_half_float)
    adapter_up_weight = jnp.einsum(
        "yg,ghi->yhi", task_selector, all_tasks_up, preferred_element_type=single_float
    ).astype(brain_half_float)
    rank = adapter_down_weight.shape[1]
    whole = lax.all_gather(tokens, "tensor", axis=0, tiled=True)
    rows_all, model_width = whole.shape
    block = rows_all // per_group
    rows_dev = rows_all // n_shards
    block_inputs = whole.reshape(per_group, block, model_width)
    input_columns = lax.dynamic_slice_in_dim(block_inputs, shard * width, width, 2)
    frozen_output = jnp.dot(whole, w_query, preferred_element_type=single_float)
    down_portion = jnp.einsum(
        "grs,gps->grp", input_columns, adapter_down_weight, preferred_element_type=single_float
    )
    down_projection = lax.psum(down_portion, "tensor")
    down_low_rank = down_projection.astype(brain_half_float)
    low_rank_update = jnp.einsum(
        "elm,emn->eln", down_low_rank, adapter_up_weight, preferred_element_type=single_float
    ).reshape(rows_all, width)
    output = (frozen_output + low_rank_update).astype(brain_half_float)
    block_output_grads = cotangent.reshape(per_group, block, width)
    backward_portion = jnp.einsum(
        "grs,gps->grp", block_output_grads, adapter_up_weight, preferred_element_type=single_float
    )
    backward_input = lax.psum(backward_portion, "tensor")
    backward_low_rank = backward_input.astype(brain_half_float)
    grad_sum = lax.psum_scatter(
        lax.dot_general(
            cotangent, w_query, (((1,), (1,)), ((), ())), preferred_element_type=single_float
        ),
        "tensor",
        scatter_dimension=0,
        tiled=True,
    )
    full_a = lax.all_gather(adapter_down_weight, "tensor", axis=2, tiled=True)
    first = shard * rows_dev
    which = first // block
    a_here = lax.dynamic_index_in_dim(full_a, which, 0, keepdims=False)
    back_rows = lax.dynamic_slice_in_dim(
        backward_low_rank.reshape(rows_all, rank), first, rows_dev, 0
    )
    grad_sum = grad_sum + jnp.dot(back_rows, a_here, preferred_element_type=single_float)
    grad_tokens = grad_sum.astype(brain_half_float)
    scale_average = 1.0 / block
    down_gradient = (
        jnp.einsum(
            "evr,evx->erx", backward_low_rank, input_columns, preferred_element_type=single_float
        )
        * scale_average
    ).astype(brain_half_float)
    up_gradient = (
        jnp.einsum(
            "evr,evx->erx", down_low_rank, block_output_grads, preferred_element_type=single_float
        )
        * scale_average
    ).astype(brain_half_float)
    task_down_weight = jnp.einsum(
        "xh,xui->hui", task_selector, down_gradient, preferred_element_type=single_float
    )
    task_up_weight = jnp.einsum(
        "xh,xui->hui", task_selector, up_gradient, preferred_element_type=single_float
    )
    own_a, own_b = (
        lax.psum_scatter(
            task_down_weight.astype(jnp.bfloat16), "dp", scatter_dimension=1, tiled=True
        ).astype(jnp.float32),
        lax.psum_scatter(
            task_up_weight.astype(jnp.bfloat16), "dp", scatter_dimension=1, tiled=True
        ).astype(jnp.float32),
    )
    hid_f = hidden.astype(single_float)
    head_grad_a = lax.dot_general(
        hid_f,
        own_a.reshape(ntasks, rank_rows * width),
        (((0,), (0,)), ((), ())),
        precision=lax.Precision.HIGHEST,
    )
    head_grad_b = lax.dot_general(
        hid_f,
        own_b.reshape(ntasks, rank_rows * width),
        (((0,), (0,)), ((), ())),
        precision=lax.Precision.HIGHEST,
    )
    grad_head_a = head_grad_a.reshape(hid_count, rank_rows, width).astype(brain_half_float)
    grad_head_b = head_grad_b.reshape(hid_count, rank_rows, width).astype(brain_half_float)
    return (output, grad_tokens, grad_head_a, grad_head_b)


def solution(mesh):
    return jax.shard_map(
        local,
        mesh=mesh,
        in_specs=(
            P(("dp", "tensor"), None),
            P(None, "tensor"),
            P("dp", "tensor"),
            P(),
            P(None, "tensor"),
            P(None, "dp", "tensor"),
            P(None, "dp", "tensor"),
            P(),
        ),
        out_specs=(
            P("dp", "tensor"),
            P(("dp", "tensor"), None),
            P(None, "dp", "tensor"),
            P(None, "dp", "tensor"),
        ),
        check_vma=False,
    )
```

profile of v0, /device:TPU:2, one launch (start us, length us, event | category | flops | bytes accessed | tf_op | source)
XLA Modules:
  0.0 520.4 jit_solution(2591239751184445774)
XLA Ops:
  7.2 0.0 copy-start
  7.2 0.0 all-gather.9.cloned.1.call-start
  7.2 1.2 multiply_convert_fusion.2
  8.4 20.3 %all_gather.16 = bf16[128,512]{0,1:T(8,128)(2,1)S(1)} all-gather(bf16[128,32]{0,1:T(8,128)(2,1)S(1)} %multiply_convert_fusion.2), channel_id=1, replica_groups=mesh['dp'=16,'tensor'=16] {'tensor'}, dimensions={1}, use_global_device_ids=true | all-gather | bytes 139264 | tf_op jit(solution)/shard_map/all_gather | solution.py:21
  28.8 2.0 convolution_convert_fusion.3
  30.7 0.0 all-gather.9.cloned.1.call-update
  30.7 0.0 all-gather.11.cloned.1.call-start
  30.8 2.0 convolution_convert_fusion.2
  32.7 0.0 all-gather.11.cloned.1.call-update
  32.8 0.0 all-gather.7.cloned.1.call-start
  32.8 0.7 all-gather.7.cloned.1.call-update
  33.5 0.0 reduce-scatter.10.cloned.1.call-start
  33.6 1.2 dynamic_slice.11
  34.8 0.6 fusion.29
  35.5 45.3 %all-gather.9.cloned.1.call-done = bf16[128,8192]{1,0:T(8,128)(2,1)} async-done(((bf16[128,512]{1,0:T(8,128)(2,1)}), bf16[128,8192]{1,0:T(8,128)(2,1)}) %all-gather.9.cloned.1.call-update) | async-done | bytes 2097168 | tf_op jit(solution)/shard_map/all_gather | solution.py:37
  80.7 2.6 fusion.4
  83.3 51.8 %all-gather.11.cloned.1.call-done = bf16[128,8192]{1,0:T(8,128)(2,1)} async-done(((bf16[128,512]{1,0:T(8,128)(2,1)}), bf16[128,8192]{1,0:T(8,128)(2,1)}) %all-gather.11.cloned.1.call-update) | async-done | bytes 2097168 | tf_op jit(solution)/shard_map/all_gather | solution.py:38
  135.2 2.6 fusion.1
  137.8 0.0 copy-done
  137.8 0.2 convolution_bitcast_fusion
  138.0 54.6 %all-gather.7.cloned.1.call-done = bf16[512,8192]{1,0:T(8,128)(2,1)} async-done(((bf16[32,8192]{1,0:T(8,128)(2,1)}), bf16[512,8192]{1,0:T(8,128)(2,1)}) %all-gather.7.cloned.1.call-update) | async-done | bytes 8388624 | tf_op jit(solution)/shard_map/all_gather | solution.py:48
  192.6 1.3 convolution_bitcast_fusion.1
  193.9 46.9 %all-reduce.2 = (bf16[1,512,16]{1,2,0:T(8,128)(2,1)S(1)}, bf16[1,512,16]{1,2,0:T(8,128)(2,1)S(1)}) all-reduce(f32[1,512,16]{1,2,0:T(8,128)S(1)} %convolution_bitcast_fusion.1, f32[1,512,16]{1,2,0:T(8,128)S(1)} %convolution_bitcast_fusion), channel_id=1, replica_groups=mesh['dp'=16,'tensor'=16] {'tensor'}, use_global_device_ids=true, to_apply=%region_0.1 | all-reduce | flops 16384 | bytes 98304 | tf_op jit(solution)/shard_map/psum | solution.py:58
  240.8 0.2 fusion.13
  240.9 1.2 fusion.11
  242.2 3.5 multiply_convert_fusion
  245.6 0.0 reduce-scatter.10.cloned.1.call-update
  245.7 0.0 reduce-scatter.12.cloned.1.call-start
  245.7 0.5 reduce-scatter.12.cloned.1.call-update
  246.3 0.0 reduce-scatter.8.cloned.1.call-start
  246.3 11.6 %fusion.36 = f32[512,8192]{1,0:T(8,128)} fusion(bf16[512,512]{1,0:T(8,128)(2,1)S(1)} %copy-done, bf16[8192,512]{1,0:T(8,128)(2,1)} %param.9), kind=kOutput, calls=%fused_computation.52 | convolution fusion | flops 4294967296 | bytes 25690112 | tf_op jit(solution)/shard_map/dot_general | solution.py:71
  257.9 0.0 reduce-scatter.8.cloned.1.call-update
  257.9 14.9 %all-gather.2 = bf16[16,8192]{1,0:T(8,128)(2,1)S(1)} all-gather(bf16[16,512]{1,0:T(8,128)(2,1)S(1)} %bitcast.73), channel_id=4, replica_groups=mesh['dp'=16,'tensor'=16] {'tensor'}, dimensions={1}, use_global_device_ids=true | all-gather | bytes 278528 | tf_op jit(solution)/shard_map/all_gather | solution.py:78
  272.8 9.5 %fusion.35 = f32[512,512]{1,0:T(8,128)S(1)} fusion(bf16[512,8192]{1,0:T(8,128)(2,1)} %all-gather.7.cloned.1.call-done, bf16[8192,512]{1,0:T(8,128)(2,1)} %param.9), kind=kOutput, calls=%fused_computation.51 | convolution fusion | flops 4294967296 | bytes 17825792 | tf_op jit(solution)/shard_map/dot_general | solution.py:54
  282.3 1.1 fusion.7
  283.4 42.0 %reduce-scatter.10.cloned.1.call-done = bf16[128,1,512]{2,0,1:T(8,128)(2,1)} async-done(((bf16[128,16,512]{2,0,1:T(8,128)(2,1)}), bf16[128,1,512]{2,0,1:T(8,128)(2,1)}) %reduce-scatter.10.cloned.1.call-update) | async-done | bytes 131088
  325.4 2.0 fusion.8
  327.4 81.0 %reduce-scatter.12.cloned.1.call-done = bf16[128,1,512]{2,0,1:T(8,128)(2,1)} async-done(((bf16[128,16,512]{2,0,1:T(8,128)(2,1)}), bf16[128,1,512]{2,0,1:T(8,128)(2,1)}) %reduce-scatter.12.cloned.1.call-update) | async-done | bytes 131088
  408.5 2.0 fusion.9
  410.4 100.7 %reduce-scatter.8.cloned.1.call-done = f32[32,8192]{1,0:T(8,128)} async-done(((f32[512,8192]{1,0:T(8,128)}), f32[32,8192]{1,0:T(8,128)}) %reduce-scatter.8.cloned.1.call-update) | async-done | bytes 1048592 | tf_op jit(solution)/shard_map/reduce_scatter | solution.py:70
  511.1 2.4 fusion
  (1 shorter events, 0.0 us)
Async XLA Ops:
  7.2 130.6 %copy-start = (bf16[512,512]{1,0:T(8,128)(2,1)S(1)}, bf16[512,512]{1,0:T(8,128)(2,1)}, u32[]{:S(2)}) copy-start(bf16[512,512]{1,0:T(8,128)(2,1)} %param.10) | copy-start | bytes 1572868
  7.2 73.5 %all-gather.9.cloned.1.call-start = ((), (), s32[]{:S(2)}) async-start(), calls=%async_computation.5 | async-start | bytes 2228224 | tf_op jit(solution)/shard_map/all_gather | solution.py:37
  30.7 104.4 %all-gather.11.cloned.1.call-start = ((), (), s32[]{:S(2)}) async-start(), calls=%async_computation.6 | async-start | bytes 2228224 | tf_op jit(solution)/shard_map/all_gather | solution.py:38
  32.8 159.8 %all-gather.7.cloned.1.call-start = ((), (), s32[]{:S(2)}) async-start(), calls=%async_computation.3 | async-start | bytes 8912896 | tf_op jit(solution)/shard_map/all_gather | solution.py:48
  33.5 291.9 %reduce-scatter.10.cloned.1.call-start = ((), (), s32[]{:S(2)}) async-start(), calls=%async_computation.7 | async-start | bytes 2228224
  245.7 162.8 %reduce-scatter.12.cloned.1.call-start = ((), (), s32[]{:S(2)}) async-start(), calls=%async_computation.8 | async-start | bytes 2228224
  246.3 264.9 %reduce-scatter.8.cloned.1.call-start = ((), (), s32[]{:S(2)}) async-start(), calls=%async_computation.4 | async-start | bytes 17825792 | tf_op jit(solution)/shard_map/reduce_scatter | solution.py:70
Sparse Core Ops, SparseCore 0:
  30.9 49.8 all-gather.8
  83.7 51.4 all-gather.10
  137.0 55.5 all-gather.6
  245.8 79.6 reduce-scatter.9
  328.8 79.5 reduce-scatter.11
  410.9 100.2 reduce-scatter.7
where the time goes:
time: 521 us; the launch traced here: 520 us
  waiting for transfers between devices  377 us (72%)
  blocking collectives  82.1 us (16%)
  matrix products  41.8 us (8%)
  between operations  14.2 us (3%)
    unnamed x8, waiting for transfers between devices  124 us
    reduce_scatter x1, waiting for transfers between devices, local(): lax.psum_scatter(lax.dot_general(cotangent, w_query, (((1,), (1,)), ((),...  101 us
    all_gather x1, waiting for transfers between devices, local(): whole = lax.all_gather(tokens, 'tensor', axis=0, tiled=True)  54.6 us
    all_gather x1, waiting for transfers between devices, local(): lax.all_gather(gen_b, 'dp', axis=1, tiled=True)  51.8 us
    psum x1, blocking collectives, local(): down_projection = lax.psum(down_portion, 'tensor')  46.9 us
    all_gather x1, waiting for transfers between devices, local(): lax.all_gather(gen_a, 'dp', axis=1, tiled=True)  45.3 us
    all_gather x1, blocking collectives, local(): hidden = lax.all_gather(hid_part, 'tensor', axis=1, tiled=True)  20.3 us
    all_gather x1, blocking collectives, local(): full_a = lax.all_gather(adapter_down_weight, 'tensor', axis=2, tiled=True)  14.9 us
  transfers between devices with their start and end apart: 6, of which 6 were waited for; matrix products, arithmetic and copies ran while one was open for 7% of the time, Pallas kernels for 0%

commit v1 on v0

--- a/solution.py
+++ b/solution.py
@@ -2,6 +2,9 @@
 import jax.numpy as jnp
 from jax import lax
 from jax.sharding import PartitionSpec as P
+from jax.lax import all_gather
+
+render_halves = lambda array_here: all_gather(array_here, axis_name="tensor").sum(axis=0)
 
 
 def local(tokens, w_query, cotangent, task_embed, w_hidden, head_a, head_b, block_task):
@@ -55,7 +58,7 @@
     down_portion = jnp.einsum(
         "grs,gps->grp", input_columns, adapter_down_weight, preferred_element_type=single_float
     )
-    down_projection = lax.psum(down_portion, "tensor")
+    down_projection = render_halves(down_portion)
     down_low_rank = down_projection.astype(brain_half_float)
     low_rank_update = jnp.einsum(
         "elm,emn->eln", down_low_rank, adapter_up_weight, preferred_element_type=single_float

time: 521 us -> 492 us (0.944)
  waiting for transfers between devices: 377 us -> 326 us
  blocking collectives: 82.1 us -> 104 us
    all_gather x1, waiting for transfers between devices: 54.6 us -> 4.11 us  [local(): whole = lax.all_gather(tokens, 'tensor', axis=0, tiled=True)]
    all_gather x0 -> x1, blocking collectives: none -> 16.9 us  [all_gather(array_here, axis_name='tensor').sum(axis=0)]
where the time goes in v1:
time: 492 us; the launch traced here: 491 us
  waiting for transfers between devices  326 us (66%)
  blocking collectives  104 us (21%)
  matrix products  41.8 us (8%)
  between operations  14.2 us (3%)
    unnamed x8, waiting for transfers between devices  124 us
    reduce_scatter x1, waiting for transfers between devices, local(): lax.psum_scatter(lax.dot_general(cotangent, w_query, (((1,), (1,)), ((),...  101 us
    all_gather x1, waiting for transfers between devices, local(): lax.all_gather(gen_b, 'dp', axis=1, tiled=True)  51.8 us
    psum x1, blocking collectives, local(): backward_input = lax.psum(backward_portion, 'tensor')  51 us
    all_gather x1, waiting for transfers between devices, local(): lax.all_gather(gen_a, 'dp', axis=1, tiled=True)  45.3 us
    all_gather x1, blocking collectives, local(): hidden = lax.all_gather(hid_part, 'tensor', axis=1, tiled=True)  20.3 us
    all_gather x1, blocking collectives, all_gather(array_here, axis_name='tensor').sum(axis=0)  16.9 us
    all_gather x1, blocking collectives, local(): full_a = lax.all_gather(adapter_down_weight, 'tensor', axis=2, tiled=True)  15.4 us
  transfers between devices with their start and end apart: 6, of which 6 were waited for; matrix products, arithmetic and copies ran while one was open for 7% of the time, Pallas kernels for 0%

profile of v1, /device:TPU:2, one launch (start us, length us, event | category | flops | bytes accessed | tf_op | source)
XLA Modules:
  0.0 491.3 jit_solution(15709266019836484573)
XLA Ops:
  7.2 0.0 copy-start
  7.2 0.0 all-gather.10.cloned.1.call-start
  7.2 1.2 multiply_convert_fusion.2
  8.4 20.3 %all_gather.22 = bf16[128,512]{0,1:T(8,128)(2,1)S(1)} all-gather(bf16[128,32]{0,1:T(8,128)(2,1)S(1)} %multiply_convert_fusion.2), channel_id=1, replica_groups=mesh['dp'=16,'tensor'=16] {'tensor'}, dimensions={1}, use_global_device_ids=true | all-gather | bytes 139264 | tf_op jit(solution)/shard_map/all_gather | solution.py:24
  28.8 2.0 convolution_convert_fusion.3
  30.7 0.0 all-gather.10.cloned.1.call-update
  30.7 0.0 all-gather.12.cloned.1.call-start
  30.8 2.0 convolution_convert_fusion.2
  32.7 0.0 all-gather.12.cloned.1.call-update
  32.8 0.0 all-gather.8.cloned.1.call-start
  32.8 0.7 all-gather.8.cloned.1.call-update
  33.5 0.0 reduce-scatter.10.cloned.1.call-start
  33.6 1.2 dynamic_slice.11
  34.8 0.6 fusion.28
  35.5 45.3 %all-gather.10.cloned.1.call-done = bf16[128,8192]{1,0:T(8,128)(2,1)} async-done(((bf16[128,512]{1,0:T(8,128)(2,1)}), bf16[128,8192]{1,0:T(8,128)(2,1)}) %all-gather.10.cloned.1.call-update) | async-done | bytes 2097168 | tf_op jit(solution)/shard_map/all_gather | solution.py:40
  80.7 2.6 fusion.4
  83.3 51.8 %all-gather.12.cloned.1.call-done = bf16[128,8192]{1,0:T(8,128)(2,1)} async-done(((bf16[128,512]{1,0:T(8,128)(2,1)}), bf16[128,8192]{1,0:T(8,128)(2,1)}) %all-gather.12.cloned.1.call-update) | async-done | bytes 2097168 | tf_op jit(solution)/shard_map/all_gather | solution.py:41
  135.2 2.6 fusion.1
  137.8 0.0 copy-done
  137.8 0.2 convolution_bitcast_fusion
  138.0 51.0 %psum.7 = bf16[1,512,16]{1,2,0:T(8,128)(2,1)S(1)} all-reduce(f32[1,512,16]{1,2,0:T(8,128)S(1)} %convolution_bitcast_fusion), channel_id=1, replica_groups=mesh['dp'=16,'tensor'=16] {'tensor'}, use_global_device_ids=true, to_apply=%region_2.3 | all-reduce | flops 8192 | bytes 49152 | tf_op jit(solution)/shard_map/psum | solution.py:71
  189.1 4.1 all-gather.8.cloned.1.call-done
  193.2 1.3 fusion.17
  194.4 16.9 %all-gather.1 = f32[8192,16]{0,1:T(8,128)S(1)} all-gather(f32[512,16]{0,1:T(8,128)S(1)} %fusion.17), channel_id=3, replica_groups=mesh['dp'=16,'tensor'=16] {'tensor'}, dimensions={0}, use_global_device_ids=true | all-gather | bytes 557056 | tf_op jit(solution)/shard_map/all_gather | solution.py:7
  211.3 0.3 copy.18
  211.6 0.1 bitcast_reduce_fusion
  211.7 0.2 fusion.13
  211.9 1.2 fusion.11
  213.1 3.5 multiply_convert_fusion
  216.6 0.0 reduce-scatter.10.cloned.1.call-update
  216.6 0.0 reduce-scatter.12.cloned.1.call-start
  216.6 0.5 reduce-scatter.12.cloned.1.call-update
  217.2 0.0 reduce-scatter.8.cloned.1.call-start
  217.2 11.6 %fusion.35 = f32[512,8192]{1,0:T(8,128)} fusion(bf16[512,512]{1,0:T(8,128)(2,1)S(1)} %copy-done, bf16[8192,512]{1,0:T(8,128)(2,1)} %param.9), kind=kOutput, calls=%fused_computation.51 | convolution fusion | flops 4294967296 | bytes 25690112 | tf_op jit(solution)/shard_map/dot_general | solution.py:74
  228.8 0.0 reduce-scatter.8.cloned.1.call-update
  228.9 15.4 %all-gather.3 = bf16[16,8192]{1,0:T(8,128)(2,1)S(1)} all-gather(bf16[16,512]{1,0:T(8,128)(2,1)S(1)} %bitcast.74), channel_id=5, replica_groups=mesh['dp'=16,'tensor'=16] {'tensor'}, dimensions={1}, use_global_device_ids=true | all-gather | bytes 278528 | tf_op jit(solution)/shard_map/all_gather | solution.py:81
  244.3 9.5 %fusion.34 = f32[512,512]{1,0:T(8,128)S(1)} fusion(bf16[512,8192]{1,0:T(8,128)(2,1)} %all-gather.8.cloned.1.call-done, bf16[8192,512]{1,0:T(8,128)(2,1)} %param.9), kind=kOutput, calls=%fused_computation.50 | convolution fusion | flops 4294967296 | bytes 17825792 | tf_op jit(solution)/shard_map/dot_general | solution.py:57
  253.8 1.1 fusion.7
  254.9 41.4 %reduce-scatter.10.cloned.1.call-done = bf16[128,1,512]{2,0,1:T(8,128)(2,1)} async-done(((bf16[128,16,512]{2,0,1:T(8,128)(2,1)}), bf16[128,1,512]{2,0,1:T(8,128)(2,1)}) %reduce-scatter.10.cloned.1.call-update) | async-done | bytes 131088
  296.3 2.0 fusion.8
  298.3 81.1 %reduce-scatter.12.cloned.1.call-done = bf16[128,1,512]{2,0,1:T(8,128)(2,1)} async-done(((bf16[128,16,512]{2,0,1:T(8,128)(2,1)}), bf16[128,1,512]{2,0,1:T(8,128)(2,1)}) %reduce-scatter.12.cloned.1.call-update) | async-done | bytes 131088
  379.4 2.0 fusion.9
  381.3 100.7 %reduce-scatter.8.cloned.1.call-done = f32[32,8192]{1,0:T(8,128)} async-done(((f32[512,8192]{1,0:T(8,128)}), f32[32,8192]{1,0:T(8,128)}) %reduce-scatter.8.cloned.1.call-update) | async-done | bytes 1048592 | tf_op jit(solution)/shard_map/reduce_scatter | solution.py:73
  482.1 2.4 fusion
  (1 shorter events, 0.0 us)
Async XLA Ops:
  7.2 130.6 %copy-start = (bf16[512,512]{1,0:T(8,128)(2,1)S(1)}, bf16[512,512]{1,0:T(8,128)(2,1)}, u32[]{:S(2)}) copy-start(bf16[512,512]{1,0:T(8,128)(2,1)} %param.10) | copy-start | bytes 1572868
  7.2 73.5 %all-gather.10.cloned.1.call-start = ((), (), s32[]{:S(2)}) async-start(), calls=%async_computation.5 | async-start | bytes 2228224 | tf_op jit(solution)/shard_map/all_gather | solution.py:40
  30.7 104.4 %all-gather.12.cloned.1.call-start = ((), (), s32[]{:S(2)}) async-start(), calls=%async_computation.6 | async-start | bytes 2228224 | tf_op jit(solution)/shard_map/all_gather | solution.py:41
  32.8 160.4 %all-gather.8.cloned.1.call-start = ((), (), s32[]{:S(2)}) async-start(), calls=%async_computation.3 | async-start | bytes 8912896 | tf_op jit(solution)/shard_map/all_gather | solution.py:51
  33.5 262.8 %reduce-scatter.10.cloned.1.call-start = ((), (), s32[]{:S(2)}) async-start(), calls=%async_computation.7 | async-start | bytes 2228224
  216.6 162.8 %reduce-scatter.12.cloned.1.call-start = ((), (), s32[]{:S(2)}) async-start(), calls=%async_computation.8 | async-start | bytes 2228224
  217.2 264.9 %reduce-scatter.8.cloned.1.call-start = ((), (), s32[]{:S(2)}) async-start(), calls=%async_computation.4 | async-start | bytes 17825792 | tf_op jit(solution)/shard_map/reduce_scatter | solution.py:73
Sparse Core Ops, SparseCore 0:
  30.9 49.8 all-gather.9
  83.7 51.4 all-gather.11
  137.0 56.1 all-gather.7
  216.7 79.5 reduce-scatter.9
  299.7 79.6 reduce-scatter.11
  381.8 100.2 reduce-scatter.7
